TPU v7x, 32 devices: a whole 2x2x4 slice. The times are simulated.
32 devices in a mesh: fsdp: 4 (over y, core), ctx: 4 (over z), uly: 2 (over x).
Axes of the slice: x: 2, y: 2, z: 4, core: 2. Of those that a mesh axis runs over, the one named last changes fastest.
Arguments:
- query_states: bfloat16 [12, 384, 8192], P('fsdp', 'ctx', 'uly'), may hold values from -8 to 8
- key_projections: bfloat16 [12, 384, 1024], P('fsdp', 'ctx', 'uly'), may hold values from -8 to 8
- value_projections: bfloat16 [12, 384, 1024], P('fsdp', 'ctx', 'uly'), may hold values from -6 to 6
- layer_bias: bfloat16 [10240], P('fsdp'), may hold values from -3 to 3
- positions: int32 [12, 384], P('fsdp', 'ctx'), may hold values from 0 to 383, as said below
- rescale: float32 [2, 64], replicated, may hold values from 1 to 16
- table_index: int32 [12], P('fsdp'), may hold values from 0 to 1
Outputs:
- attended: bfloat16 [12, 384, 8192], P('fsdp', 'ctx', 'uly')
Inputs may be any that keep to these rules, and one draw needn't show every extreme that they name: In each sequence the rows come in aligned runs of 48; every run holds 48 consecutive positions in increasing order, starting at a multiple of 48, and every position 0 to 383 occurs once. The order of the runs differs between sequences.
All inputs are finite; a program needn't handle non-finite values.
Results may differ from a plain program's by a relative error of at most 0.012.
Values may be sent and summed in bfloat16 or wider, within the bound.
A program may use at most 64 MiB of HBM per device.

v0:
```python
import math

import jax
import jax.numpy as jnp
from jax import lax
from jax.sharding import PartitionSpec as P

QUERY_HEADS = 64
KEY_VALUE_HEADS = 8
HEAD_SIZE = 128


rope_base = 1000000.0
masked_value = -1e30


def apply_rotation(states, positions, scale_factors):
    half_dim = states.shape[-1] // 2
    exponent = jnp.arange(half_dim, dtype=jnp.float32) * (2.0 / states.shape[-1])
    inverse = 1.0 / (scale_factors * jnp.power(jnp.float32(rope_base), exponent)[None, :])
    angles = positions.astype(jnp.float32)[:, :, None] * inverse[:, None, :]
    cosine = jnp.cos(angles)[:, :, None, :]
    sine_wave = jnp.sin(angles)[:, :, None, :]
    leading = states[..., :half_dim]
    trailing = states[..., half_dim:]
    return jnp.concatenate(
        [leading * cosine - trailing * sine_wave, trailing * cosine + leading * sine_wave], axis=-1
    )


def make_folder(query_grouped, query_positions, key_heads_here):

    def attend(running, block_piece):
        highest, totals, weighted_blend = running
        block_keys, block_values, block_positions = block_piece
        key_rows = block_keys.reshape(-1, key_heads_here, HEAD_SIZE)
        value_rows = block_values.reshape(-1, key_heads_here, HEAD_SIZE)
        scores = jnp.einsum(
            "qgrd,kgd->grqk", query_grouped, key_rows, preferred_element_type=jnp.float32
        ) / math.sqrt(HEAD_SIZE)
        allowed = block_positions[0][None, :] <= query_positions[0][:, None]
        block_high = jnp.max(jnp.where(allowed, scores, masked_value), axis=-1)
        new_high = jnp.maximum(highest, block_high)
        weights = jnp.where(allowed, jnp.exp(scores - new_high[..., None]), 0.0)
        shrink = jnp.exp(highest - new_high)
        totals = jnp.sum(weights, axis=-1)
        weighted_blend = jnp.einsum(
            "grqk,kgd->grqd",
            weights.astype(jnp.bfloat16),
            value_rows,
            preferred_element_type=jnp.float32,
        )
        return (new_high, totals, weighted_blend)

    def folder(running, block_piece, offset):
        return attend(running, block_piece)

    return folder


def initial_state(key_heads_here, group_fraction, query_rows):
    return (
        jnp.full((key_heads_here, group_fraction, query_rows), masked_value, jnp.float32),
        jnp.zeros((key_heads_here, group_fraction, query_rows), jnp.float32),
        jnp.zeros((key_heads_here, group_fraction, query_rows, HEAD_SIZE), jnp.float32),
    )


def finish(running, query_rows):
    highest, totals, weighted_blend = running
    normalized = weighted_blend / totals[..., None]
    return normalized.transpose(2, 0, 1, 3).reshape(1, query_rows, -1).astype(jnp.bfloat16)


def on_device(
    query_states, key_projections, value_projections, layer_bias, positions, rescale, table_index
):
    bias_terms = lax.all_gather(layer_bias, "fsdp", axis=0, tiled=True).astype(jnp.float32)
    local_count = query_states.shape[0]
    tokens_here = query_states.shape[1]
    query_heads_here = query_states.shape[2] // HEAD_SIZE
    key_heads_here = key_projections.shape[2] // HEAD_SIZE
    uly_place = lax.axis_index("uly")
    query_span_width = QUERY_HEADS * HEAD_SIZE
    key_span_width = KEY_VALUE_HEADS * HEAD_SIZE
    query_bias = lax.dynamic_slice_in_dim(
        bias_terms[:query_span_width].reshape(QUERY_HEADS, HEAD_SIZE),
        uly_place * query_heads_here,
        query_heads_here,
        0,
    )
    key_offset_bias = lax.dynamic_slice_in_dim(
        bias_terms[query_span_width : query_span_width + key_span_width].reshape(
            KEY_VALUE_HEADS, HEAD_SIZE
        ),
        uly_place * key_heads_here,
        key_heads_here,
        0,
    )
    value_offset_bias = lax.dynamic_slice_in_dim(
        bias_terms[query_span_width + key_span_width :].reshape(KEY_VALUE_HEADS, HEAD_SIZE),
        uly_place * key_heads_here,
        key_heads_here,
        0,
    )
    selector = (
        jnp.arange(rescale.shape[0], dtype=jnp.int32)[None, :] == table_index[:, None]
    ).astype(jnp.float32)
    scale_factors = jnp.dot(selector, rescale, precision=lax.Precision.HIGHEST)
    query_rotated_all = apply_rotation(
        query_states.astype(jnp.float32).reshape(
            local_count, tokens_here, query_heads_here, HEAD_SIZE
        )
        + query_bias,
        positions,
        scale_factors,
    )
    query_rotated_all = query_rotated_all.astype(jnp.bfloat16).reshape(
        local_count, tokens_here, query_heads_here * HEAD_SIZE
    )
    key_rotated_all = apply_rotation(
        key_projections.astype(jnp.float32).reshape(
            local_count, tokens_here, key_heads_here, HEAD_SIZE
        )
        + key_offset_bias,
        positions,
        scale_factors,
    )
    key_rotated_all = key_rotated_all.astype(jnp.bfloat16).reshape(
        local_count, tokens_here, key_heads_here * HEAD_SIZE
    )
    value_all = (
        value_projections.astype(jnp.float32).reshape(
            local_count, tokens_here, key_heads_here, HEAD_SIZE
        )
        + value_offset_bias
    ).astype(jnp.bfloat16)
    value_all = value_all.reshape(local_count, tokens_here, key_heads_here * HEAD_SIZE)
    group_fraction = QUERY_HEADS // KEY_VALUE_HEADS
    results = []
    for member in range(local_count):
        query_rotated_rows = query_rotated_all[member : member + 1]
        key_rotated_rows = key_rotated_all[member : member + 1]
        value_with_bias = value_all[member : member + 1]
        member_positions = positions[member : member + 1]
        query_grouped = query_rotated_rows.reshape(
            tokens_here, key_heads_here, group_fraction, HEAD_SIZE
        )
        folder = make_folder(query_grouped, member_positions, key_heads_here)
        running = folder(
            initial_state(key_heads_here, group_fraction, tokens_here),
            (
                lax.all_gather(key_rotated_rows, "ctx", axis=1, tiled=True),
                lax.all_gather(value_with_bias, "ctx", axis=1, tiled=True),
                lax.all_gather(member_positions, "ctx", axis=1, tiled=True),
            ),
            jnp.int32(0),
        )
        results.append(finish(running, tokens_here))
    return jnp.concatenate(results, axis=0)


def solution(mesh):
    in_specs = (
        P("fsdp", "ctx", "uly"),
        P("fsdp", "ctx", "uly"),
        P("fsdp", "ctx", "uly"),
        P("fsdp"),
        P("fsdp", "ctx"),
        P(),
        P("fsdp"),
    )
    out_specs = P("fsdp", "ctx", "uly")
    return jax.shard_map(
        on_device, mesh=mesh, in_specs=in_specs, out_specs=out_specs, check_vma=False
    )
```

profile of v0, /device:TPU:0, one launch (start us, length us, event | category | flops | bytes accessed | tf_op | source)
XLA Modules:
  0.0 148.7 jit_solution(562633976710418100)
XLA Ops:
  0.9 6.2 %all-gather = bf16[4,1,2560]{2,1,0:T(2,128)(2,1)S(1)} all-gather(bf16[1,1,2560]{2,1,0:T(2,128)(2,1)S(1)} %reshape.188), channel_id=1, replica_groups=mesh['fsdp'=4,'ctx'=4,'uly'=2] {'fsdp'}, dimensions={0}, use_global_device_ids=true | all-gather | bytes 25600 | tf_op jit(solution)/shard_map/all_gather | solution.py:78
  8.4 1.1 reshape.174
  13.4 15.4 %all_gather.32 = bf16[1,384,512]{2,1,0:T(8,128)(2,1)S(1)} all-gather(bf16[1,96,512]{2,1,0:T(8,128)(2,1)S(1)} %slice.114), channel_id=1, replica_groups=mesh['fsdp'=4,'ctx'=4,'uly'=2] {'ctx'}, dimensions={1}, use_global_device_ids=true | all-gather | bytes 491520 | tf_op jit(solution)/shard_map/all_gather | solution.py:153
  30.4 1.7 %subtract_convert_fusion = (bf16[3,96,32,64]{3,1,2,0:T(8,128)(2,1)S(1)}, bf16[3,96,32,64]{3,1,2,0:T(8,128)(2,1)S(1)}) fusion(f32[3,96,32,128]{3,1,2,0:T(8,128)S(1)} %bitcast_add_fusion, f32[3,96,64]{2,1,0:T(8,128)S(1)} %get-tuple-element.24, f32[3,96,64]{2,1,0:T(8,128)S(1)} %get-tuple-element.23), kind=kLoop, calls=%fused_computation.18 | loop fusion | flops 4718592 | bytes 7225344 | tf_op jit(solution)/shard_map/convert.3
  32.1 1.3 fusion.44
  35.0 9.2 %all-reduce.3 = (s32[384]{0:T(512)}, s32[384]{0:T(512)}, s32[384]{0:T(512)S(1)}) all-reduce(s32[384]{0:T(512)S(1)} %fusion.56, s32[384]{0:T(512)S(1)} %fusion.55, s32[384]{0:T(512)S(1)} %fusion.54), channel_id=1, replica_groups=mesh['fsdp'=4,'ctx'=4,'uly'=2] {'ctx'}, use_global_device_ids=true, to_apply=%add.2 | all-reduce | flops 1152 | bytes 9216
  44.3 1.0 fusion.6
  45.3 2.1 %copy-done.1 = f32[4,384,96,8]{1,2,3,0:T(8,128)} copy-done((f32[4,384,96,8]{1,2,3,0:T(8,128)}, f32[4,384,96,8]{1,2,3,0:T(8,128)S(1)}, u32[]{:S(2)}) %copy-start.1) | copy-done | bytes 4718616
  47.5 1.6 %fusion.9 = f32[4,8,96]{2,1,0:T(8,128)S(1)} fusion(f32[4,384,96,8]{1,2,3,0:T(8,128)S(1)} %get-tuple-element.33, f32[4,8,96]{2,1,0:T(8,128)S(1)} %broadcast_maximum_fusion.2, pred[96,384]{1,0:T(8,128)(4,1)S(1)} %broadcast_compare_fusion.2), kind=kLoop, calls=%fused_computation.19 | loop fusion | flops 4715520 | bytes 4780032 | tf_op jit(solution)/shard_map/reduce_sum | solution.py:46
  49.5 15.1 %all_gather.33 = bf16[1,384,512]{2,1,0:T(8,128)(2,1)S(1)} all-gather(bf16[1,96,512]{2,1,0:T(8,128)(2,1)S(1)} %slice.123), channel_id=1, replica_groups=mesh['fsdp'=4,'ctx'=4,'uly'=2] {'ctx'}, dimensions={1}, use_global_device_ids=true | all-gather | bytes 491520 | tf_op jit(solution)/shard_map/all_gather | solution.py:154
  64.9 3.7 %fusion.35 = bf16[96,4,8,128]{3,0,2,1:T(8,128)(2,1)S(1)} fusion(bf16[384,4,128,1]{0,2,3,1:T(8,128)(2,1)S(1)} %bitcast.148, f32[4,384,96,8]{1,2,3,0:T(8,128)} %copy-done.1, f32[4,8,96]{2,1,0:T(8,128)S(1)} %broadcast_maximum_fusion.2, pred[96,384]{1,0:T(8,128)(4,1)S(1)} %broadcast_compare_fusion.2, f32[96,4,8]{0,2,1:T(8,128)S(1)} %bitcast.151), kind=kOutput, calls=%fused_computation.50 | convolution fusion | flops 307494912 | bytes 5959680 | tf_op jit(solution)/shard_map/grqk,kgd->grqd/dot_general | solution.py:47
  69.3 14.4 %all_gather.35 = bf16[1,384,512]{2,1,0:T(8,128)(2,1)S(1)} all-gather(bf16[1,96,512]{2,1,0:T(8,128)(2,1)S(1)} %slice.126), channel_id=1, replica_groups=mesh['fsdp'=4,'ctx'=4,'uly'=2] {'ctx'}, dimensions={1}, use_global_device_ids=true | all-gather | bytes 491520 | tf_op jit(solution)/shard_map/all_gather | solution.py:153
  84.1 1.0 fusion.3
  85.1 2.1 %copy-done.3 = f32[4,384,96,8]{1,2,3,0:T(8,128)} copy-done((f32[4,384,96,8]{1,2,3,0:T(8,128)}, f32[4,384,96,8]{1,2,3,0:T(8,128)S(1)}, u32[]{:S(2)}) %copy-start.3) | copy-done | bytes 4718616
  87.2 1.6 %fusion.11 = f32[4,8,96]{2,1,0:T(8,128)S(1)} fusion(f32[4,384,96,8]{1,2,3,0:T(8,128)S(1)} %get-tuple-element.31, f32[4,8,96]{2,1,0:T(8,128)S(1)} %broadcast_maximum_fusion.1, pred[96,384]{1,0:T(8,128)(4,1)S(1)} %broadcast_compare_fusion.1), kind=kLoop, calls=%fused_computation.21 | loop fusion | flops 4715520 | bytes 4780032 | tf_op jit(solution)/shard_map/reduce_sum | solution.py:46
  88.9 14.4 %all_gather.36 = bf16[1,384,512]{2,1,0:T(8,128)(2,1)S(1)} all-gather(bf16[1,96,512]{2,1,0:T(8,128)(2,1)S(1)} %slice.129), channel_id=1, replica_groups=mesh['fsdp'=4,'ctx'=4,'uly'=2] {'ctx'}, dimensions={1}, use_global_device_ids=true | all-gather | bytes 491520 | tf_op jit(solution)/shard_map/all_gather | solution.py:154
  103.5 3.7 %fusion.34 = bf16[96,4,8,128]{3,0,2,1:T(8,128)(2,1)S(1)} fusion(bf16[384,4,128,1]{0,2,3,1:T(8,128)(2,1)S(1)} %bitcast.149, f32[4,384,96,8]{1,2,3,0:T(8,128)} %copy-done.3, f32[4,8,96]{2,1,0:T(8,128)S(1)} %broadcast_maximum_fusion.1, pred[96,384]{1,0:T(8,128)(4,1)S(1)} %broadcast_compare_fusion.1, f32[96,4,8]{0,2,1:T(8,128)S(1)} %bitcast.153), kind=kOutput, calls=%fused_computation.48 | convolution fusion | flops 307494912 | bytes 5959680 | tf_op jit(solution)/shard_map/grqk,kgd->grqd/dot_general | solution.py:47
  107.9 15.1 %all_gather.38 = bf16[1,384,512]{2,1,0:T(8,128)(2,1)S(1)} all-gather(bf16[1,96,512]{2,1,0:T(8,128)(2,1)S(1)} %slice.132), channel_id=1, replica_groups=mesh['fsdp'=4,'ctx'=4,'uly'=2] {'ctx'}, dimensions={1}, use_global_device_ids=true | all-gather | bytes 491520 | tf_op jit(solution)/shard_map/all_gather | solution.py:153
  123.4 1.0 fusion
  124.4 2.1 %copy-done.2 = f32[4,384,96,8]{1,2,3,0:T(8,128)} copy-done((f32[4,384,96,8]{1,2,3,0:T(8,128)}, f32[4,384,96,8]{1,2,3,0:T(8,128)S(1)}, u32[]{:S(2)}) %copy-start.2) | copy-done | bytes 4718616
  126.5 1.6 %fusion.13 = f32[4,8,96]{2,1,0:T(8,128)S(1)} fusion(f32[4,384,96,8]{1,2,3,0:T(8,128)S(1)} %get-tuple-element.29, f32[4,8,96]{2,1,0:T(8,128)S(1)} %broadcast_maximum_fusion, pred[96,384]{1,0:T(8,128)(4,1)S(1)} %broadcast_compare_fusion), kind=kLoop, calls=%fused_computation.23 | loop fusion | flops 4715520 | bytes 4780032 | tf_op jit(solution)/shard_map/reduce_sum | solution.py:46
  128.2 14.3 %all_gather.39 = bf16[1,384,512]{2,1,0:T(8,128)(2,1)S(1)} all-gather(bf16[1,96,512]{2,1,0:T(8,128)(2,1)S(1)} %slice.135), channel_id=1, replica_groups=mesh['fsdp'=4,'ctx'=4,'uly'=2] {'ctx'}, dimensions={1}, use_global_device_ids=true | all-gather | bytes 491520 | tf_op jit(solution)/shard_map/all_gather | solution.py:154
  142.7 3.7 %fusion.33 = bf16[96,4,8,128]{3,0,2,1:T(8,128)(2,1)S(1)} fusion(bf16[384,4,128,1]{0,2,3,1:T(8,128)(2,1)S(1)} %bitcast.150, f32[4,384,96,8]{1,2,3,0:T(8,128)} %copy-done.2, f32[4,8,96]{2,1,0:T(8,128)S(1)} %broadcast_maximum_fusion, pred[96,384]{1,0:T(8,128)(4,1)S(1)} %broadcast_compare_fusion, f32[96,4,8]{0,2,1:T(8,128)S(1)} %bitcast.152), kind=kOutput, calls=%fused_computation.46 | convolution fusion | flops 307494912 | bytes 5959680 | tf_op jit(solution)/shard_map/grqk,kgd->grqd/dot_general | solution.py:47
  147.0 1.7 %pad_maximum_fusion = bf16[3,96,4096]{2,1,0:T(8,128)(2,1)} fusion(bf16[1,96,4096]{2,1,0:T(8,128)(2,1)S(1)} %convert_element_type.78, bf16[1,96,4096]{2,1,0:T(8,128)(2,1)S(1)} %convert_element_type.75, bf16[1,96,4096]{2,1,0:T(8,128)(2,1)S(1)} %convert_element_type.72), kind=kLoop, calls=%fused_computation.28 | loop fusion | flops 2359296 | bytes 4718592 | tf_op jit(solution)/shard_map/concatenate | solution.py:160
  (69 shorter events, 12.4 us)
Async XLA Ops:
  0.0 9.6 %copy-start = (f32[2,64]{1,0:T(2,128)S(1)}, f32[2,64]{1,0:T(2,128)}, u32[]{:S(2)}) copy-start(f32[2,64]{1,0:T(2,128)} %param.12) | copy-start | bytes 1540
  0.0 29.8 %copy-start.4 = (bf16[3,96,4096]{2,1,0:T(8,128)(2,1)S(1)}, bf16[3,96,4096]{2,1,0:T(8,128)(2,1)}, u32[]{:S(2)}) copy-start(bf16[3,96,4096]{2,1,0:T(8,128)(2,1)} %param.7) | copy-start | bytes 7077892
  32.1 1.3 copy-start.10
  32.1 2.6 %copy-start.7 = (s32[3,96]{1,0:T(4,128)S(1)}, s32[3,96]{1,0:T(4,128)}, u32[]{:S(2)}) copy-start(s32[3,96]{1,0:T(4,128)} %param.11) | copy-start | bytes 3460
  44.3 4.8 %copy-start.6 = (bf16[3,96,512]{2,1,0:T(8,128)(2,1)S(1)}, bf16[3,96,512]{2,1,0:T(8,128)(2,1)}, u32[]{:S(2)}) copy-start(bf16[3,96,512]{2,1,0:T(8,128)(2,1)} %param.9) | copy-start | bytes 884740
  45.3 2.1 %copy-start.1 = (f32[4,384,96,8]{1,2,3,0:T(8,128)}, f32[4,384,96,8]{1,2,3,0:T(8,128)S(1)}, u32[]{:S(2)}) copy-start(f32[4,384,96,8]{1,2,3,0:T(8,128)S(1)} %get-tuple-element.33) | copy-start | bytes 14155780
  64.9 4.4 %copy-start.5 = (bf16[1,96,4,128]{3,2,1,0:T(4,128)(2,1)S(1)}, bf16[1,96,4,128]{3,2,1,0:T(4,128)(2,1)}, u32[]{:S(2)}) copy-start(bf16[1,96,4,128]{3,2,1,0:T(4,128)(2,1)} %get-tuple-element.17) | copy-start | bytes 294916
  64.9 19.1 %copy-start.9 = (s32[384]{0:T(512)S(1)}, s32[384]{0:T(512)}, u32[]{:S(2)}) copy-start(s32[384]{0:T(512)} %get-tuple-element.6) | copy-start | bytes 4612
  85.1 2.1 %copy-start.3 = (f32[4,384,96,8]{1,2,3,0:T(8,128)}, f32[4,384,96,8]{1,2,3,0:T(8,128)S(1)}, u32[]{:S(2)}) copy-start(f32[4,384,96,8]{1,2,3,0:T(8,128)S(1)} %get-tuple-element.31) | copy-start | bytes 14155780
  103.5 19.7 %copy-start.8 = (s32[384]{0:T(512)S(1)}, s32[384]{0:T(512)}, u32[]{:S(2)}) copy-start(s32[384]{0:T(512)} %get-tuple-element.5) | copy-start | bytes 4612
  124.4 2.1 %copy-start.2 = (f32[4,384,96,8]{1,2,3,0:T(8,128)}, f32[4,384,96,8]{1,2,3,0:T(8,128)S(1)}, u32[]{:S(2)}) copy-start(f32[4,384,96,8]{1,2,3,0:T(8,128)S(1)} %get-tuple-element.29) | copy-start | bytes 14155780
where the time goes:
time: 149 us
  blocking collectives  104 us (70%)
  matrix products  15.1 us (10%)
  local copies, waits for them, and re-layouts  14.5 us (10%)
  other arithmetic  14 us (9%)
    all_gather x3, blocking collectives, on_device(): lax.all_gather(key_rotated_rows, 'ctx', axis=1, tiled=True)  44.9 us
    all_gather x3, blocking collectives, on_device(): lax.all_gather(value_with_bias, 'ctx', axis=1, tiled=True)  43.8 us
    dot_general x3, matrix products, attend(): jnp.einsum('grqk,kgd->grqd', weights.astype(jnp.bfloat16), value_rows, pr...  11.1 us
    unnamed x1, blocking collectives  9.2 us
    unnamed x32, local copies, waits for them, and re-layouts  8.12 us
    all_gather x1, blocking collectives, on_device(): lax.all_gather(layer_bias, 'fsdp', axis=0, tiled=True).astype(jnp.float32)  6.2 us
    reduce_sum x3, other arithmetic, attend(): totals = jnp.sum(weights, axis=-1)  4.82 us
    dot_general x3, matrix products, attend(): jnp.einsum('qgrd,kgd->grqk', query_grouped, key_rows, preferred_element_t...  3.1 us

commit v1 on v0

v1 whole, which is shorter than its diff:
```python
import functools
import math

import jax
import jax.numpy as jnp
from jax import lax
from jax.experimental import pallas as pl
from jax.experimental.pallas import tpu as pltpu
from jax.sharding import PartitionSpec as P

QUERY_HEADS = 64
KEY_VALUE_HEADS = 8
HEAD_SIZE = 128
GROUP = QUERY_HEADS // KEY_VALUE_HEADS
RUN = 48

rope_base = 1000000.0
masked_value = -1e30
MESH = pl.DeviceIdType.MESH


def sine_cosine(angle):
    turns = jnp.floor(angle * (2.0 / math.pi) + 0.5)
    r = angle - turns * 1.5703125
    r = r - turns * 4.837512969970703125e-4
    r = r - turns * 7.54978995489188216e-8
    z = r * r
    s = r + r * z * (-1.6666654611e-1 + z * (8.3321608736e-3 - z * 1.9515295891e-4))
    c = 1.0 - 0.5 * z + z * z * (
        4.166664568298827e-2 + z * (-1.388731625493765e-3 + z * 2.443315711809948e-5)
    )
    quarter = turns.astype(jnp.int32) & 3
    odd = (quarter & 1) == 1
    sine = jnp.where(odd, c, s)
    cosine = jnp.where(odd, s, c)
    sine = jnp.where(quarter >= 2, -sine, sine)
    cosine = jnp.where((quarter == 1) | (quarter == 2), -cosine, cosine)
    return sine, cosine


def kernel(
    n, nf, ahead, rows_at_once,
    table_ref, q_hbm, k_hbm, v_hbm, bias_in, pos_in, rescale_ref,
    out_hbm,
    q_buf, q_rot, kv, out_buf, cos_t, sin_t, mask_t, pos_buf, bias_buf, bias_f,
    q_sem, own_sem, send_right, send_left, recv_sem,
    pos_send, pos_recv, bias_send, bias_recv, out_sem,
):
    batch, rows, _ = q_hbm.shape
    heads_kv = k_hbm.shape[2] // HEAD_SIZE
    units = batch * heads_kv
    me = lax.axis_index("ctx")
    mf = lax.axis_index("fsdp")
    mu = lax.axis_index("uly")
    shard_rows = bias_in.shape[0]
    wide = GROUP * HEAD_SIZE

    def own_copies(u):
        b, g = u // heads_kv, u % heads_kv
        lanes = pl.ds(g * HEAD_SIZE, HEAD_SIZE)
        return (
            pltpu.make_async_copy(k_hbm.at[b, :, lanes], kv.at[me, u, 0], own_sem.at[u, 0]),
            pltpu.make_async_copy(v_hbm.at[b, :, lanes], kv.at[me, u, 1], own_sem.at[u, 1]),
        )

    for u in range(units):
        for copy in own_copies(u):
            copy.start()

    def q_copy(b):
        return pltpu.make_async_copy(q_hbm.at[b], q_buf.at[b], q_sem.at[b])

    barrier = pltpu.get_barrier_semaphore()
    for d in range(1, n):
        pl.semaphore_signal(
            barrier, inc=1, device_id={"ctx": lax.rem(me + d, n)}, device_id_type=MESH
        )
    for d in range(1, nf):
        pl.semaphore_signal(
            barrier, inc=1, device_id={"fsdp": lax.rem(mf + d, nf)}, device_id_type=MESH
        )
    for b in range(batch):
        q_copy(b).start()
    pos_buf[me] = pos_in[...]
    bias_buf[mf] = bias_in[...]
    for u in range(units):
        for copy in own_copies(u):
            copy.wait()
    pl.semaphore_wait(barrier, n - 1 + nf - 1)

    def pos_copy(d):
        return pltpu.make_async_remote_copy(
            src_ref=pos_in, dst_ref=pos_buf.at[me],
            send_sem=pos_send.at[d], recv_sem=pos_recv.at[d],
            device_id={"ctx": lax.rem(me + d, n)}, device_id_type=MESH,
        )

    def bias_copy(d):
        return pltpu.make_async_remote_copy(
            src_ref=bias_in, dst_ref=bias_buf.at[mf],
            send_sem=bias_send.at[d], recv_sem=bias_recv.at[d],
            device_id={"fsdp": lax.rem(mf + d, nf)}, device_id_type=MESH,
        )

    def to_right(shard, u):
        return pltpu.make_async_remote_copy(
            src_ref=kv.at[shard, u], dst_ref=kv.at[shard, u],
            send_sem=send_right.at[shard, u], recv_sem=recv_sem.at[shard, u],
            device_id={"ctx": lax.rem(me + 1, n)}, device_id_type=MESH,
        )

    def to_left(shard, u):
        return pltpu.make_async_remote_copy(
            src_ref=kv.at[shard, u], dst_ref=kv.at[shard, u],
            send_sem=send_left.at[shard, u], recv_sem=recv_sem.at[shard, u],
            device_id={"ctx": lax.rem(me + n - 1, n)}, device_id_type=MESH,
        )

    def send_own(u):
        @pl.when(me < n - 1)
        def _():
            to_right(me, u).start()

        @pl.when(me > 0)
        def _():
            to_left(me, u).start()

    for d in range(1, n):
        pos_copy(d).start()
    for d in range(1, nf):
        bias_copy(d).start()
    for u in range(min(ahead, units)):
        send_own(u)

    for d in range(1, nf):
        bias_copy(d).wait_recv()
    for f in range(nf):
        bias_f[f] = bias_buf[f].astype(jnp.float32)

    def bias_row(row):
        return bias_f[row // shard_rows, pl.ds(row % shard_rows, 1), :]

    for d in range(1, n):
        pos_copy(d).wait_recv()

    lane = lax.broadcasted_iota(jnp.int32, (1, HEAD_SIZE), 1)
    power = jnp.exp(
        (lane % (HEAD_SIZE // 2)).astype(jnp.float32)
        * (2.0 / HEAD_SIZE * math.log(rope_base))
    )
    low_half = lane < HEAD_SIZE // 2
    run_rows = lax.broadcasted_iota(jnp.int32, (RUN, HEAD_SIZE), 0)
    keys = n * rows
    key_lane = lax.broadcasted_iota(jnp.int32, (1, keys), 1)
    query_row = lax.broadcasted_iota(jnp.int32, (RUN, 1), 0)
    for b in range(batch):
        factors = rescale_ref[0:1, :]
        for t in range(1, rescale_ref.shape[0]):
            factors = jnp.where(table_ref[b] == t, rescale_ref[t : t + 1, :], factors)
        inverse = 1.0 / (jnp.concatenate([factors, factors], axis=1) * power)

        key_pos = key_lane % RUN
        for j in range(n):
            for piece in range(rows // RUN):
                first = pos_buf[j, b : b + 1, piece * RUN : piece * RUN + 1]
                here = key_lane // RUN == j * (rows // RUN) + piece
                key_pos = key_pos + jnp.where(here, first, 0)
                place = (run_rows + first).astype(jnp.float32)
                sine, cosine = sine_cosine(place * inverse)
                block = slice(piece * RUN, (piece + 1) * RUN)
                cos_t[b, j, block, :] = cosine
                sin_t[b, j, block, :] = jnp.where(low_half, -sine, sine)
        for piece in range(rows // RUN):
            first = pos_in[b : b + 1, piece * RUN : piece * RUN + 1]
            allowed = key_pos <= query_row + first
            mask_t[b, piece * RUN : (piece + 1) * RUN, :] = jnp.where(
                allowed, 0.0, masked_value
            )

    def rotate(x, cosine, sine):
        return x * cosine + pltpu.roll(x, HEAD_SIZE // 2, 1) * sine

    query_heads_here = heads_kv * GROUP
    for b in range(batch):
        q_copy(b).wait()

        @pl.loop(0, heads_kv)
        def _(g):
            for i in range(GROUP):
                x = q_buf[
                    b, :, pl.ds(pl.multiple_of(g * wide + i * HEAD_SIZE, HEAD_SIZE), HEAD_SIZE)
                ].astype(jnp.float32)
                x = x + bias_row(mu * query_heads_here + g * GROUP + i)
                q_rot[b * heads_kv + g, i * rows : (i + 1) * rows, :] = rotate(
                    x, cos_t[b, me], sin_t[b, me]
                ).astype(jnp.bfloat16)

    scale = math.log2(math.e) / math.sqrt(HEAD_SIZE)

    def out_copy(u):
        b, g = u // heads_kv, u % heads_kv
        return pltpu.make_async_copy(
            out_buf.at[u],
            out_hbm.at[b, :, pl.ds(pl.multiple_of(g * wide, wide), wide)],
            out_sem.at[u],
        )

    def compute(u):
        b, g = u // heads_kv, u % heads_kv
        k_bias = bias_row(QUERY_HEADS + mu * heads_kv + g)
        v_bias = bias_row(QUERY_HEADS + KEY_VALUE_HEADS + mu * heads_kv + g)
        k_parts, v_parts = [], []
        for j in range(n):
            x = kv[j, u, 0].astype(jnp.float32) + k_bias
            k_parts.append(rotate(x, cos_t[b, j], sin_t[b, j]).astype(jnp.bfloat16))
            v_parts.append((kv[j, u, 1].astype(jnp.float32) + v_bias).astype(jnp.bfloat16))
        k_all = jnp.concatenate(k_parts, axis=0)
        v_all = jnp.concatenate(v_parts, axis=0)
        mask = mask_t[b]
        heads_at_once = rows_at_once
        for i in range(0, GROUP, heads_at_once):
            q = q_rot[u, i * rows : (i + heads_at_once) * rows, :]
            s = lax.dot_general(
                q, k_all, (((1,), (1,)), ((), ())), preferred_element_type=jnp.float32
            )
            s = s.reshape(heads_at_once, rows, keys) + mask[None]
            high = jnp.max(s, axis=-1, keepdims=True)
            p = jnp.exp2((s - high) * scale)
            total = jnp.sum(p, axis=-1, keepdims=True)
            o = jnp.dot(
                p.astype(jnp.bfloat16).reshape(heads_at_once * rows, keys), v_all,
                preferred_element_type=jnp.float32,
            ).reshape(heads_at_once, rows, HEAD_SIZE)
            o = (o / total).astype(jnp.bfloat16)
            for e in range(heads_at_once):
                out_buf[u, :, (i + e) * HEAD_SIZE : (i + e + 1) * HEAD_SIZE] = o[e]
        out_copy(u).start()

    lag = n - 2

    @pl.loop(0, units + lag)
    def _(t):
        @pl.when(t + ahead < units)
        def _():
            send_own(t + ahead)

        for hop in range(1, n):
            u = t - hop + 1

            @pl.when((u >= 0) & (u < units) & (me + hop < n))
            def _():
                to_left(me + hop, u).wait_recv()

                @pl.when(me > 0)
                def _():
                    to_left(me + hop, u).start()

            @pl.when((u >= 0) & (u < units) & (me - hop >= 0))
            def _():
                to_right(me - hop, u).wait_recv()

                @pl.when(me < n - 1)
                def _():
                    to_right(me - hop, u).start()

        @pl.when(t >= lag)
        def _():
            compute(t - lag)

    @pl.loop(0, units)
    def _(u):
        out_copy(u).wait()
        for j in range(n):
            @pl.when((j <= me) & (me < n - 1))
            def _():
                to_right(j, u).wait_send()

            @pl.when((j >= me) & (me > 0))
            def _():
                to_left(j, u).wait_send()

    for d in range(1, n):
        pos_copy(d).wait_send()
    for d in range(1, nf):
        bias_copy(d).wait_send()


def on_device(n, nf, q, k, v, bias, positions, rescale, table_index):
    batch, rows, width = q.shape
    heads_kv = k.shape[2] // HEAD_SIZE
    units = batch * heads_kv
    keys = n * rows
    bias = bias.reshape(-1, HEAD_SIZE)
    any_spec = pl.BlockSpec(memory_space=pl.ANY)
    vmem = pl.BlockSpec(memory_space=pltpu.VMEM)
    dma = pltpu.SemaphoreType.DMA
    return pl.pallas_call(
        functools.partial(kernel, n, nf, 3, 4 if n <= 4 else 1),
        out_shape=jax.ShapeDtypeStruct(q.shape, jnp.bfloat16),
        in_specs=[
            pl.BlockSpec(memory_space=pltpu.SMEM), any_spec, any_spec, any_spec, vmem, vmem, vmem,
        ],
        out_specs=any_spec,
        scratch_shapes=[
            pltpu.VMEM((batch, rows, width), jnp.bfloat16),
            pltpu.VMEM((units, GROUP * rows, HEAD_SIZE), jnp.bfloat16),
            pltpu.VMEM((n, units, 2, rows, HEAD_SIZE), jnp.bfloat16),
            pltpu.VMEM((units, rows, GROUP * HEAD_SIZE), jnp.bfloat16),
            pltpu.VMEM((batch, n, rows, HEAD_SIZE), jnp.float32),
            pltpu.VMEM((batch, n, rows, HEAD_SIZE), jnp.float32),
            pltpu.VMEM((batch, rows, keys), jnp.float32),
            pltpu.VMEM((n,) + positions.shape, jnp.int32),
            pltpu.VMEM((nf,) + bias.shape, jnp.bfloat16),
            pltpu.VMEM((nf,) + bias.shape, jnp.float32),
            dma((batch,)), dma((units, 2)),
            dma((n, units)), dma((n, units)), dma((n, units)),
            dma((n,)), dma((n,)), dma((nf,)), dma((nf,)), dma((units,)),
        ],
        compiler_params=pltpu.CompilerParams(
            collective_id=0, has_side_effects=True, vmem_limit_bytes=48 * 1024 * 1024
        ),
        name="relay_attention",
    )(table_index, q, k, v, bias, positions, rescale)


def solution(mesh):
    in_specs = (
        P("fsdp", "ctx", "uly"),
        P("fsdp", "ctx", "uly"),
        P("fsdp", "ctx", "uly"),
        P("fsdp"),
        P("fsdp", "ctx"),
        P(),
        P("fsdp"),
    )
    n, nf = mesh.shape["ctx"], mesh.shape["fsdp"]
    return jax.shard_map(
        functools.partial(on_device, n, nf),
        mesh=mesh, in_specs=in_specs, out_specs=P("fsdp", "ctx", "uly"), check_vma=False,
    )
```

time: 149 us -> 60 us (0.40)
  blocking collectives: 104 us -> 0 us
  Pallas kernels: 0 us -> 52 us
  matrix products: 15.1 us -> 0 us
  other arithmetic: 14 us -> 0 us
  local copies, waits for them, and re-layouts: 14.5 us -> 7.7 us
    all_gather x7 -> x0, blocking collectives: 94.9 us -> none  [the longest x3 44.9 us: on_device(): lax.all_gather(key_rotated_rows, 'ctx', axis=1, tiled=True)]
    pallas_call x0 -> x1, Pallas kernels: none -> 52 us  [on_device(): pl.pallas_call(functools.partial(kernel, n, nf, 3, 4 if n <= 4 else 1), o...]
    dot_general x7 -> x0, matrix products: 15.1 us -> none  [the longest x3 11.1 us: attend(): jnp.einsum('grqk,kgd->grqd', weights.astype(jnp.bfloat16), value_rows, pr...]
    unnamed x1 -> x0, blocking collectives: 9.2 us -> none
    reduce_sum x3 -> x0, other arithmetic: 4.82 us -> none  [attend(): totals = jnp.sum(weights, axis=-1)]
    concatenate x3 -> x0, other arithmetic: 3.99 us -> none  [the longest x2 2.32 us: apply_rotation(): jnp.concatenate([leading * cosine - trailing * sine_wave, trailing * cosi...]
    another operation x5 -> x0, other arithmetic: 2.28 us -> none
    convert_element_type x6 -> x0, local copies, waits for them, and re-layouts: 1.92 us -> none  [finish(): normalized.transpose(2, 0, 1, 3).reshape(1, query_rows, -1)]
where the time goes in v1:
time: 60 us; the launch traced here: 59.7 us
  Pallas kernels  52 us (87%)
  local copies, waits for them, and re-layouts  7.7 us (13%)
    pallas_call x1, Pallas kernels, on_device(): pl.pallas_call(functools.partial(kernel, n, nf, 3, 4 if n <= 4 else 1), o...  52 us
    unnamed x15, local copies, waits for them, and re-layouts  7.7 us

profile of v1, /device:TPU:0, one launch (start us, length us, event | category | flops | bytes accessed | tf_op | source)
XLA Modules:
  0.0 59.7 jit_solution(7319515307867280572)
XLA Ops:
  0.0 0.0 copy-start
  0.0 1.7 %copy-done = bf16[3,96,4096]{2,1,0:T(8,128)(2,1)S(1)} copy-done((bf16[3,96,4096]{2,1,0:T(8,128)(2,1)S(1)}, bf16[3,96,4096]{2,1,0:T(8,128)(2,1)}, u32[]{:S(2)}) %copy-start) | copy-done | bytes 2359320
  1.7 0.0 copy-start.1
  1.7 1.0 %copy-done.1 = bf16[3,96,512]{2,1,0:T(8,128)(2,1)S(1)} copy-done((bf16[3,96,512]{2,1,0:T(8,128)(2,1)S(1)}, bf16[3,96,512]{2,1,0:T(8,128)(2,1)}, u32[]{:S(2)}) %copy-start.1) | copy-done | bytes 294936
  2.6 0.0 copy-start.2
  2.6 1.0 %copy-done.2 = bf16[3,96,512]{2,1,0:T(8,128)(2,1)S(1)} copy-done((bf16[3,96,512]{2,1,0:T(8,128)(2,1)S(1)}, bf16[3,96,512]{2,1,0:T(8,128)(2,1)}, u32[]{:S(2)}) %copy-start.2) | copy-done | bytes 294936
  3.6 0.0 copy-start.3
  3.6 0.7 %copy-done.3 = bf16[2560]{0:T(1024)(128)(2,1)S(1)} copy-done((bf16[2560]{0:T(1024)(128)(2,1)S(1)}, bf16[2560]{0:T(1024)(128)(2,1)}, u32[]{:S(2)}) %copy-start.3) | copy-done | bytes 5144
  4.3 0.0 copy-start.4
  4.3 0.7 %copy-done.4 = s32[3,96]{1,0:T(4,128)S(1)} copy-done((s32[3,96]{1,0:T(4,128)S(1)}, s32[3,96]{1,0:T(4,128)}, u32[]{:S(2)}) %copy-start.4) | copy-done | bytes 1176
  5.0 0.0 copy-start.5
  5.0 0.7 %copy-done.5 = f32[2,64]{1,0:T(2,128)S(1)} copy-done((f32[2,64]{1,0:T(2,128)S(1)}, f32[2,64]{1,0:T(2,128)}, u32[]{:S(2)}) %copy-start.5) | copy-done | bytes 536
  5.6 0.0 copy-start.6
  5.6 0.7 %copy-done.6 = s32[3]{0:T(128)S(1)} copy-done((s32[3]{0:T(128)S(1)}, s32[3]{0:T(128)}, u32[]{:S(2)}) %copy-start.6) | copy-done | bytes 36
  6.3 52.0 %relay_attention.1 = bf16[3,96,4096]{2,1,0:T(8,128)(2,1)S(1)} custom-call(s32[3]{0:T(128)S(1)} %copy-done.6, bf16[3,96,4096]{2,1,0:T(8,128)(2,1)S(1)} %copy-done, bf16[3,96,512]{2,1,0:T(8,128)(2,1)S(1)} %copy-done.1, bf16[3,96,512]{2,1,0:T(8,128)(2,1)S(1)} %copy-done.2, bf16[20,128]{1,0:T(8,128)(2,1)S(1)} %bitcast.1, s32[3,96]{1,0:T(4,128)S(1)} %copy-done.4, ...), custom_call_target="tpu_custom_call" | custom-call | tf_op jit(solution)/shard_map/relay_attention/pallas_call | solution.py:297
  58.3 1.4 %copy.9 = bf16[3,96,4096]{2,1,0:T(8,128)(2,1)} copy(bf16[3,96,4096]{2,1,0:T(8,128)(2,1)S(1)} %relay_attention.1) | data formatting | bytes 4718592
Async XLA Ops:
  0.0 1.7 %copy-start = (bf16[3,96,4096]{2,1,0:T(8,128)(2,1)S(1)}, bf16[3,96,4096]{2,1,0:T(8,128)(2,1)}, u32[]{:S(2)}) copy-start(bf16[3,96,4096]{2,1,0:T(8,128)(2,1)} %q_hbm.1) | copy-start | bytes 7077892
  1.7 1.0 %copy-start.1 = (bf16[3,96,512]{2,1,0:T(8,128)(2,1)S(1)}, bf16[3,96,512]{2,1,0:T(8,128)(2,1)}, u32[]{:S(2)}) copy-start(bf16[3,96,512]{2,1,0:T(8,128)(2,1)} %k_hbm.1) | copy-start | bytes 884740
  2.6 1.0 %copy-start.2 = (bf16[3,96,512]{2,1,0:T(8,128)(2,1)S(1)}, bf16[3,96,512]{2,1,0:T(8,128)(2,1)}, u32[]{:S(2)}) copy-start(bf16[3,96,512]{2,1,0:T(8,128)(2,1)} %v_hbm.1) | copy-start | bytes 884740
  3.6 0.7 %copy-start.3 = (bf16[2560]{0:T(1024)(128)(2,1)S(1)}, bf16[2560]{0:T(1024)(128)(2,1)}, u32[]{:S(2)}) copy-start(bf16[2560]{0:T(1024)(128)(2,1)} %param.10) | copy-start | bytes 15364
  4.3 0.7 %copy-start.4 = (s32[3,96]{1,0:T(4,128)S(1)}, s32[3,96]{1,0:T(4,128)}, u32[]{:S(2)}) copy-start(s32[3,96]{1,0:T(4,128)} %pos_in.1) | copy-start | bytes 3460
  5.0 0.7 %copy-start.5 = (f32[2,64]{1,0:T(2,128)S(1)}, f32[2,64]{1,0:T(2,128)}, u32[]{:S(2)}) copy-start(f32[2,64]{1,0:T(2,128)} %rescale_ref.1) | copy-start | bytes 1540
  5.6 0.7 %copy-start.6 = (s32[3]{0:T(128)S(1)}, s32[3]{0:T(128)}, u32[]{:S(2)}) copy-start(s32[3]{0:T(128)} %table_ref.1) | copy-start | bytes 40

commit v2 on v1

--- a/solution.py
+++ b/solution.py
@@ -39,12 +39,13 @@
 
 
 def kernel(
-    n, nf, ahead, rows_at_once,
-    table_ref, q_hbm, k_hbm, v_hbm, bias_in, pos_in, rescale_ref,
-    out_hbm,
-    q_buf, q_rot, kv, out_buf, cos_t, sin_t, mask_t, pos_buf, bias_buf, bias_f,
+    n, nf, heads_at_once,
+    table_hbm, q_hbm, k_hbm, v_hbm, bias_hbm, pos_hbm, rescale_hbm,
+    out_ref,
+    table_ref, bias_in, pos_in, rescale_ref, small_sem,
+    q_buf, q_rot, kv, cos_t, sin_t, mask_t, pos_buf, bias_buf, bias_f,
     q_sem, own_sem, send_right, send_left, recv_sem,
-    pos_send, pos_recv, bias_send, bias_recv, out_sem,
+    pos_send, pos_recv, bias_send, bias_recv,
 ):
     batch, rows, _ = q_hbm.shape
     heads_kv = k_hbm.shape[2] // HEAD_SIZE
@@ -55,6 +56,27 @@
     shard_rows = bias_in.shape[0]
     wide = GROUP * HEAD_SIZE
 
+    barrier = pltpu.get_barrier_semaphore()
+    for d in range(1, n):
+        pl.semaphore_signal(
+            barrier, inc=1, device_id={"ctx": lax.rem(me + d, n)}, device_id_type=MESH
+        )
+    for d in range(1, nf):
+        pl.semaphore_signal(
+            barrier, inc=1, device_id={"fsdp": lax.rem(mf + d, nf)}, device_id_type=MESH
+        )
+    small = [
+        pltpu.make_async_copy(source, target, small_sem.at[i])
+        for i, (source, target) in enumerate(
+            (
+                (pos_hbm, pos_in), (bias_hbm, bias_in),
+                (rescale_hbm, rescale_ref), (table_hbm, table_ref),
+            )
+        )
+    ]
+    for copy in small:
+        copy.start()
+
     def own_copies(u):
         b, g = u // heads_kv, u % heads_kv
         lanes = pl.ds(g * HEAD_SIZE, HEAD_SIZE)
@@ -70,22 +92,12 @@
     def q_copy(b):
         return pltpu.make_async_copy(q_hbm.at[b], q_buf.at[b], q_sem.at[b])
 
-    barrier = pltpu.get_barrier_semaphore()
-    for d in range(1, n):
-        pl.semaphore_signal(
-            barrier, inc=1, device_id={"ctx": lax.rem(me + d, n)}, device_id_type=MESH
-        )
-    for d in range(1, nf):
-        pl.semaphore_signal(
-            barrier, inc=1, device_id={"fsdp": lax.rem(mf + d, nf)}, device_id_type=MESH
-        )
     for b in range(batch):
         q_copy(b).start()
+    for copy in small:
+        copy.wait()
     pos_buf[me] = pos_in[...]
     bias_buf[mf] = bias_in[...]
-    for u in range(units):
-        for copy in own_copies(u):
-            copy.wait()
     pl.semaphore_wait(barrier, n - 1 + nf - 1)
 
     def pos_copy(d):
@@ -129,7 +141,9 @@
         pos_copy(d).start()
     for d in range(1, nf):
         bias_copy(d).start()
-    for u in range(min(ahead, units)):
+    for u in range(units):
+        for copy in own_copies(u):
+            copy.wait()
         send_own(u)
 
     for d in range(1, nf):
@@ -197,14 +211,6 @@
 
     scale = math.log2(math.e) / math.sqrt(HEAD_SIZE)
 
-    def out_copy(u):
-        b, g = u // heads_kv, u % heads_kv
-        return pltpu.make_async_copy(
-            out_buf.at[u],
-            out_hbm.at[b, :, pl.ds(pl.multiple_of(g * wide, wide), wide)],
-            out_sem.at[u],
-        )
-
     def compute(u):
         b, g = u // heads_kv, u % heads_kv
         k_bias = bias_row(QUERY_HEADS + mu * heads_kv + g)
@@ -217,7 +223,6 @@
         k_all = jnp.concatenate(k_parts, axis=0)
         v_all = jnp.concatenate(v_parts, axis=0)
         mask = mask_t[b]
-        heads_at_once = rows_at_once
         for i in range(0, GROUP, heads_at_once):
             q = q_rot[u, i * rows : (i + heads_at_once) * rows, :]
             s = lax.dot_general(
@@ -233,17 +238,13 @@
             ).reshape(heads_at_once, rows, HEAD_SIZE)
             o = (o / total).astype(jnp.bfloat16)
             for e in range(heads_at_once):
-                out_buf[u, :, (i + e) * HEAD_SIZE : (i + e + 1) * HEAD_SIZE] = o[e]
-        out_copy(u).start()
+                start = pl.multiple_of(g * wide + (i + e) * HEAD_SIZE, HEAD_SIZE)
+                out_ref[b, :, pl.ds(start, HEAD_SIZE)] = o[e]
 
     lag = n - 2
 
     @pl.loop(0, units + lag)
     def _(t):
-        @pl.when(t + ahead < units)
-        def _():
-            send_own(t + ahead)
-
         for hop in range(1, n):
             u = t - hop + 1
 
@@ -269,7 +270,6 @@
 
     @pl.loop(0, units)
     def _(u):
-        out_copy(u).wait()
         for j in range(n):
             @pl.when((j <= me) & (me < n - 1))
             def _():
@@ -291,21 +291,22 @@
     units = batch * heads_kv
     keys = n * rows
     bias = bias.reshape(-1, HEAD_SIZE)
-    any_spec = pl.BlockSpec(memory_space=pl.ANY)
-    vmem = pl.BlockSpec(memory_space=pltpu.VMEM)
+    hbm = pl.BlockSpec(memory_space=pltpu.HBM)
     dma = pltpu.SemaphoreType.DMA
     return pl.pallas_call(
-        functools.partial(kernel, n, nf, 3, 4 if n <= 4 else 1),
+        functools.partial(kernel, n, nf, 8 if n <= 4 else 1),
         out_shape=jax.ShapeDtypeStruct(q.shape, jnp.bfloat16),
-        in_specs=[
-            pl.BlockSpec(memory_space=pltpu.SMEM), any_spec, any_spec, any_spec, vmem, vmem, vmem,
-        ],
-        out_specs=any_spec,
+        in_specs=[hbm] * 7,
+        out_specs=pl.BlockSpec(memory_space=pltpu.VMEM),
         scratch_shapes=[
+            pltpu.SMEM(table_index.shape, jnp.int32),
+            pltpu.VMEM(bias.shape, jnp.bfloat16),
+            pltpu.VMEM(positions.shape, jnp.int32),
+            pltpu.VMEM(rescale.shape, jnp.float32),
+            dma((4,)),
             pltpu.VMEM((batch, rows, width), jnp.bfloat16),
             pltpu.VMEM((units, GROUP * rows, HEAD_SIZE), jnp.bfloat16),
             pltpu.VMEM((n, units, 2, rows, HEAD_SIZE), jnp.bfloat16),
-            pltpu.VMEM((units, rows, GROUP * HEAD_SIZE), jnp.bfloat16),
             pltpu.VMEM((batch, n, rows, HEAD_SIZE), jnp.float32),
             pltpu.VMEM((batch, n, rows, HEAD_SIZE), jnp.float32),
             pltpu.VMEM((batch, rows, keys), jnp.float32),
@@ -314,13 +315,13 @@
             pltpu.VMEM((nf,) + bias.shape, jnp.float32),
             dma((batch,)), dma((units, 2)),
             dma((n, units)), dma((n, units)), dma((n, units)),
-            dma((n,)), dma((n,)), dma((nf,)), dma((nf,)), dma((units,)),
+            dma((n,)), dma((n,)), dma((nf,)), dma((nf,)),
         ],
         compiler_params=pltpu.CompilerParams(
             collective_id=0, has_side_effects=True, vmem_limit_bytes=48 * 1024 * 1024
         ),
         name="relay_attention",
-    )(table_index, q, k, v, bias, positions, rescale)
+    )(*(pltpu.with_memory_space_constraint(x, pltpu.HBM) for x in (table_index, q, k, v, bias, positions, rescale)))
 
 
 def solution(mesh):

time: 60 us -> 49 us (0.82)
  local copies, waits for them, and re-layouts: 7.7 us -> 1.41 us
  Pallas kernels: 52 us -> 47.4 us
    unnamed x15 -> x1, local copies, waits for them, and re-layouts: 7.7 us -> 1.41 us
    pallas_call x1, Pallas kernels: 52 us -> 47.4 us  [on_device(): pl.pallas_call(functools.partial(kernel, n, nf, 8 if n <= 4 else 1), out_...]
where the time goes in v2:
time: 49 us; the launch traced here: 48.8 us
  Pallas kernels  47.4 us (97%)
  local copies, waits for them, and re-layouts  1.41 us (3%)
    pallas_call x1, Pallas kernels, on_device(): pl.pallas_call(functools.partial(kernel, n, nf, 8 if n <= 4 else 1), out_...  47.4 us
    unnamed x1, local copies, waits for them, and re-layouts  1.41 us

profile of v2, /device:TPU:0, one launch (start us, length us, event | category | flops | bytes accessed | tf_op | source)
XLA Modules:
  0.0 48.8 jit_solution(148818588469602236)
XLA Ops:
  0.0 47.4 %relay_attention.1 = bf16[3,96,4096]{2,1,0:T(8,128)(2,1)S(1)} custom-call(s32[3]{0:T(128)} %table_hbm.1, bf16[3,96,4096]{2,1,0:T(8,128)(2,1)} %q_hbm.1, bf16[3,96,512]{2,1,0:T(8,128)(2,1)} %k_hbm.1, bf16[3,96,512]{2,1,0:T(8,128)(2,1)} %v_hbm.1, bf16[20,128]{1,0:T(8,128)(2,1)} %bitcast.1, s32[3,96]{1,0:T(4,128)} %pos_hbm.1, f32[2,64]{1,0:T(2,128)} %rescale_hbm.1), custom_call_target="tpu_custom_call" | custom-call | tf_op jit(solution)/shard_map/relay_attention/pallas_call | solution.py:296
  47.4 1.4 %copy.9 = bf16[3,96,4096]{2,1,0:T(8,128)(2,1)} copy(bf16[3,96,4096]{2,1,0:T(8,128)(2,1)S(1)} %relay_attention.1) | data formatting | bytes 4718592

commit v3 on v2

--- a/solution.py
+++ b/solution.py
@@ -38,6 +38,15 @@
     return sine, cosine
 
 
+def chunk_bounds(units):
+    bounds, first = [], 0
+    while first < units:
+        size = -(-(units - first) // 3)
+        bounds.append((first, size))
+        first += size
+    return bounds
+
+
 def kernel(
     n, nf, heads_at_once,
     table_hbm, q_hbm, k_hbm, v_hbm, bias_hbm, pos_hbm, rescale_hbm,
@@ -54,6 +63,7 @@
     mf = lax.axis_index("fsdp")
     mu = lax.axis_index("uly")
     shard_rows = bias_in.shape[0]
+    chunks = chunk_bounds(units)
     wide = GROUP * HEAD_SIZE
 
     barrier = pltpu.get_barrier_semaphore()
@@ -114,37 +124,40 @@
             device_id={"fsdp": lax.rem(mf + d, nf)}, device_id_type=MESH,
         )
 
-    def to_right(shard, u):
+    def to_right(shard, c):
+        part = pl.ds(*chunks[c])
         return pltpu.make_async_remote_copy(
-            src_ref=kv.at[shard, u], dst_ref=kv.at[shard, u],
-            send_sem=send_right.at[shard, u], recv_sem=recv_sem.at[shard, u],
+            src_ref=kv.at[shard, part], dst_ref=kv.at[shard, part],
+            send_sem=send_right.at[shard, c], recv_sem=recv_sem.at[shard, c],
             device_id={"ctx": lax.rem(me + 1, n)}, device_id_type=MESH,
         )
 
-    def to_left(shard, u):
+    def to_left(shard, c):
+        part = pl.ds(*chunks[c])
         return pltpu.make_async_remote_copy(
-            src_ref=kv.at[shard, u], dst_ref=kv.at[shard, u],
-            send_sem=send_left.at[shard, u], recv_sem=recv_sem.at[shard, u],
+            src_ref=kv.at[shard, part], dst_ref=kv.at[shard, part],
+            send_sem=send_left.at[shard, c], recv_sem=recv_sem.at[shard, c],
             device_id={"ctx": lax.rem(me + n - 1, n)}, device_id_type=MESH,
         )
 
-    def send_own(u):
+    def send_own(c):
         @pl.when(me < n - 1)
         def _():
-            to_right(me, u).start()
+            to_right(me, c).start()
 
         @pl.when(me > 0)
         def _():
-            to_left(me, u).start()
+            to_left(me, c).start()
 
     for d in range(1, n):
         pos_copy(d).start()
     for d in range(1, nf):
         bias_copy(d).start()
-    for u in range(units):
-        for copy in own_copies(u):
-            copy.wait()
-        send_own(u)
+    for c, (first, size) in enumerate(chunks):
+        for u in range(first, first + size):
+            for copy in own_copies(u):
+                copy.wait()
+        send_own(c)
 
     for d in range(1, nf):
         bias_copy(d).wait_recv()
@@ -243,41 +256,49 @@
 
     lag = n - 2
 
-    @pl.loop(0, units + lag)
-    def _(t):
+    def relay(step):
         for hop in range(1, n):
-            u = t - hop + 1
-
-            @pl.when((u >= 0) & (u < units) & (me + hop < n))
-            def _():
-                to_left(me + hop, u).wait_recv()
+            c = step - hop + 1
+            if c < 0 or c >= len(chunks):
+                continue
+
+            @pl.when(me + hop < n)
+            def _():
+                to_left(me + hop, c).wait_recv()
 
                 @pl.when(me > 0)
                 def _():
-                    to_left(me + hop, u).start()
-
-            @pl.when((u >= 0) & (u < units) & (me - hop >= 0))
-            def _():
-                to_right(me - hop, u).wait_recv()
+                    to_left(me + hop, c).start()
+
+            @pl.when(me - hop >= 0)
+            def _():
+                to_right(me - hop, c).wait_recv()
 
                 @pl.when(me < n - 1)
                 def _():
-                    to_right(me - hop, u).start()
-
-        @pl.when(t >= lag)
-        def _():
-            compute(t - lag)
+                    to_right(me - hop, c).start()
+
+    for step in range(lag):
+        relay(step)
 
     @pl.loop(0, units)
     def _(u):
+        for c, (first, _) in enumerate(chunks):
+            @pl.when(u == first)
+            def _():
+                relay(c + lag)
+
+        compute(u)
+
+    for c in range(len(chunks)):
         for j in range(n):
             @pl.when((j <= me) & (me < n - 1))
             def _():
-                to_right(j, u).wait_send()
+                to_right(j, c).wait_send()
 
             @pl.when((j >= me) & (me > 0))
             def _():
-                to_left(j, u).wait_send()
+                to_left(j, c).wait_send()
 
     for d in range(1, n):
         pos_copy(d).wait_send()
@@ -290,6 +311,7 @@
     heads_kv = k.shape[2] // HEAD_SIZE
     units = batch * heads_kv
     keys = n * rows
+    count = len(chunk_bounds(units))
     bias = bias.reshape(-1, HEAD_SIZE)
     hbm = pl.BlockSpec(memory_space=pltpu.HBM)
     dma = pltpu.SemaphoreType.DMA
@@ -314,7 +336,7 @@
             pltpu.VMEM((nf,) + bias.shape, jnp.bfloat16),
             pltpu.VMEM((nf,) + bias.shape, jnp.float32),
             dma((batch,)), dma((units, 2)),
-            dma((n, units)), dma((n, units)), dma((n, units)),
+            dma((n, count)), dma((n, count)), dma((n, count)),
             dma((n,)), dma((n,)), dma((nf,)), dma((nf,)),
         ],
         compiler_params=pltpu.CompilerParams(

time: 49 us -> 47.7 us (0.973)
  Pallas kernels: 47.4 us -> 46.1 us
    pallas_call x1, Pallas kernels: 47.4 us -> 46.1 us  [on_device(): pl.pallas_call(functools.partial(kernel, n, nf, 8 if n <= 4 else 1), out_...]
where the time goes in v3:
time: 47.7 us; the launch traced here: 47.5 us
  Pallas kernels  46.1 us (97%)
  local copies, waits for them, and re-layouts  1.41 us (3%)
    pallas_call x1, Pallas kernels, on_device(): pl.pallas_call(functools.partial(kernel, n, nf, 8 if n <= 4 else 1), out_...  46.1 us
    unnamed x1, local copies, waits for them, and re-layouts  1.41 us

profile of v3, /device:TPU:0, one launch (start us, length us, event | category | flops | bytes accessed | tf_op | source)
XLA Modules:
  0.0 47.5 jit_solution(14977086705048101203)
XLA Ops:
  0.0 46.1 %relay_attention.1 = bf16[3,96,4096]{2,1,0:T(8,128)(2,1)S(1)} custom-call(s32[3]{0:T(128)} %table_hbm.1, bf16[3,96,4096]{2,1,0:T(8,128)(2,1)} %q_hbm.1, bf16[3,96,512]{2,1,0:T(8,128)(2,1)} %k_hbm.1, bf16[3,96,512]{2,1,0:T(8,128)(2,1)} %v_hbm.1, bf16[20,128]{1,0:T(8,128)(2,1)} %bitcast.1, s32[3,96]{1,0:T(4,128)} %pos_hbm.1, f32[2,64]{1,0:T(2,128)} %rescale_hbm.1), custom_call_target="tpu_custom_call" | custom-call | tf_op jit(solution)/shard_map/relay_attention/pallas_call | solution.py:318
  46.1 1.4 %copy.9 = bf16[3,96,4096]{2,1,0:T(8,128)(2,1)} copy(bf16[3,96,4096]{2,1,0:T(8,128)(2,1)S(1)} %relay_attention.1) | data formatting | bytes 4718592
